TPU v7x, 32 devices: a whole 2x2x4 slice. The times are simulated.
32 devices in a mesh: pole: 2 (over x), row: 8 (over z, y), col: 2 (over core).
Axes of the slice: x: 2, y: 2, z: 4, core: 2. Of those that a mesh axis runs over, the one named last changes fastest.
Arguments:
- ancestor_inverse: float32 [2, 24576, 12288], P(None, ('pole', 'row'), 'col'), parts along dimension 1, may hold values from -6 to 6
- factor_panels: float32 [4, 2, 24576, 128], P(None, None, ('pole', 'col', 'row')), parts along dimension 2, may hold values from -0.0546875 to 0.0546875
- diag_inverse: float32 [8, 2, 128, 128], P('pole'), parts along dimension 0, may hold values from -6 to 6
- coupling: float32 [4, 2, 128, 128], P('pole'), parts along dimension 0, may hold values from -0.5 to 0.5
- block_pattern: int32 [4, 96], replicated, may hold values from 0 to 1, as said below
- tree_order: int32 [4], replicated, may hold values from 0 to 3, each once
Outputs:
- inverse_panels: float32 [4, 2, 24576, 128], P(None, None, ('pole', 'row')), parts along dimension 2
- inverse_diagonal: float32 [8, 2, 128, 128], P('pole'), parts along dimension 0
- inverse_coupling: float32 [4, 2, 128, 128], P('pole'), parts along dimension 0
There are 2 independent parts, one for each index of `pole`. A program takes and returns all parts, laid end to end along the dimension named above; an argument that names none is the same for every part. Nothing has to cross between parts.
Inputs may be any that keep to these rules, and one draw needn't show every extreme that they name: `tree_order`: each supernode number appears once. `block_pattern`: blocks 0 and 48 lie in every supernode's structure.
All inputs are finite; a program needn't handle non-finite values.
Results may differ from a plain program's by a relative error of at most 0.0001.
Values sent between devices are 32-bit elements; how exact they have to be, the bound alone decides.
A program may use at most 192 MiB of HBM per device.

v0:
```python
import jax
import jax.numpy as jnp
from jax import lax
from jax.sharding import PartitionSpec as P


def swapped(block, axis, bit):
    count = lax.axis_size(axis)
    route = []
    for low in range(count):
        high = low | 1 << bit
        if high != low and high < count:
            route += [(low, high), (high, low)]
    return lax.ppermute(block, axis, route)


def matmul(left_side, right_side):
    return jnp.dot(
        left_side, right_side, preferred_element_type=jnp.float32, precision=lax.Precision.HIGHEST
    )


def multiply(left_side, right_side):
    real_part = matmul(left_side[0], right_side[0]) - matmul(left_side[1], right_side[1])
    imag_part = matmul(left_side[0], right_side[1]) + matmul(left_side[1], right_side[0])
    return jnp.stack([real_part, imag_part])


def flipped(matrix):
    return jnp.swapaxes(matrix, 1, 2)


def row_masks(pattern_eff, first_row, row_count, block_rows):
    row_index = first_row + jnp.arange(row_count, dtype=jnp.int32)
    blocks = row_index // block_rows
    onehot = (blocks[:, None] == jnp.arange(pattern_eff.shape[1], dtype=jnp.int32)[None, :]).astype(
        jnp.float32
    )
    return matmul(pattern_eff, onehot.T)


def per_device(ancestor_inverse, factor_panels, diag_inverse, coupling, block_pattern, tree_order):
    grid_row = lax.axis_index("row")
    grid_col = lax.axis_index("col")
    tile_rows = ancestor_inverse.shape[1]
    half_rows = ancestor_inverse.shape[2]
    piece_rows = factor_panels.shape[2]
    block_rows = factor_panels.shape[3]
    super_count = factor_panels.shape[0]
    share_rows = tile_rows // 2
    sorted_pattern = jnp.take(block_pattern, tree_order, axis=0).astype(jnp.float32)
    pattern_eff = jnp.concatenate(
        [sorted_pattern[:2], sorted_pattern[2:] * sorted_pattern[:2]], axis=0
    )
    source_mask = row_masks(
        pattern_eff, grid_col * half_rows + grid_row * piece_rows, piece_rows, block_rows
    )
    target_mask = row_masks(pattern_eff, grid_row * tile_rows, tile_rows, block_rows)
    panels = jnp.take(factor_panels, tree_order, axis=0) * source_mask[:, None, :, None]
    diag_blocks = jnp.take(diag_inverse, tree_order, axis=0)
    columns = []
    products = []
    for tree_slot in range(super_count):
        gathered = lax.all_gather(panels[tree_slot], "row", axis=1, tiled=True)
        columns.append(gathered)
        products.append(lax.psum(multiply(ancestor_inverse, gathered), "col"))
    own_flag = (grid_row * tile_rows // half_rows == grid_col).astype(jnp.float32)
    offset = jnp.clip(grid_row * tile_rows - grid_col * half_rows, 0, half_rows - tile_rows)
    own_windows = jnp.stack(
        [
            lax.dynamic_slice_in_dim(column_set, offset, tile_rows, 1) * own_flag
            for column_set in columns
        ]
    )
    partner_windows = swapped(own_windows, "col", 0)
    tile_windows = own_windows + partner_windows

    def share(matrix):
        return lax.dynamic_slice_in_dim(matrix, grid_col * share_rows, share_rows, 1)

    windows = [share(tile_windows[tree_slot]) for tree_slot in range(super_count)]
    parent_cols = [
        -target_mask[tree_slot][None, :, None] * products[tree_slot] for tree_slot in range(2)
    ]
    child_cols = [
        -target_mask[tree_slot + 2][None, :, None]
        * (products[tree_slot + 2] + multiply(parent_cols[tree_slot], coupling[tree_slot]))
        for tree_slot in range(2)
    ]
    parent_local = [
        multiply(flipped(windows[tree_slot]), share(parent_cols[tree_slot]))
        for tree_slot in range(2)
    ]
    cross_local = [
        multiply(flipped(share(parent_cols[tree_slot])), windows[tree_slot + 2])
        for tree_slot in range(2)
    ]
    child_local = [
        multiply(flipped(windows[tree_slot + 2]), share(child_cols[tree_slot]))
        for tree_slot in range(2)
    ]
    parent_sums = lax.psum(jnp.stack(parent_local), ("row", "col"))
    parent_diag = [diag_blocks[tree_slot] - parent_sums[tree_slot] for tree_slot in range(2)]
    child_totals = lax.psum(jnp.stack(cross_local + child_local), ("row", "col"))
    crosses = [
        -(child_totals[tree_slot] + multiply(parent_diag[tree_slot], coupling[tree_slot]))
        for tree_slot in range(2)
    ]
    child_sums = [child_totals[2 + tree_slot] for tree_slot in range(2)]
    child_diag = [
        diag_blocks[tree_slot + 2]
        - child_sums[tree_slot]
        - multiply(flipped(coupling[tree_slot]), crosses[tree_slot])
        for tree_slot in range(2)
    ]
    all_cols = jnp.stack(parent_cols + child_cols)
    all_diag = jnp.stack(parent_diag + child_diag)
    inverse_panels = jnp.zeros_like(all_cols).at[tree_order].set(all_cols)
    inverse_diagonal = jnp.zeros_like(all_diag).at[tree_order].set(all_diag)
    return (inverse_panels, inverse_diagonal, jnp.stack(crosses))


def solution(mesh):
    return jax.shard_map(
        per_device,
        mesh=mesh,
        in_specs=(
            P(None, ("pole", "row"), "col"),
            P(None, None, ("pole", "col", "row"), None),
            P("pole", None, None, None),
            P("pole", None, None, None),
            P(),
            P(),
        ),
        out_specs=(
            P(None, None, ("pole", "row"), None),
            P("pole", None, None, None),
            P("pole", None, None, None),
        ),
        check_vma=False,
    )
```

profile of v0, /device:TPU:0, one launch (start us, length us, event | category | flops | bytes accessed | tf_op | source)
XLA Modules:
  0.0 873.5 jit_solution(7536772676169645142)
XLA Ops:
  7.2 0.8 compare_and_fusion
  9.3 1.2 gather_fusion
  10.7 2.4 gather_fusion.1
  13.5 2.4 select_multiply_fusion
  15.8 1.7 fusion.222
  19.7 99.5 %all-gather.11.cloned.1.call-done = f32[1,2,6144,128]{3,2,1,0:T(8,128)} async-done(((f32[1,2,768,128]{3,2,1,0:T(8,128)}), f32[1,2,6144,128]{3,2,1,0:T(8,128)}) %all-gather.11.cloned.1.call-update) | async-done | bytes 6291472 | tf_op jit(solution)/shard_map/all_gather | solution.py:64
  119.2 36.1 %fusion.8 = f32[128,1536]{1,0:T(8,128)S(1)} fusion(f32[2,1536,6144]{2,1,0:T(8,128)} %param.6, f32[1,2,6144,128]{3,2,1,0:T(8,128)} %all-gather.11.cloned.1.call-done), kind=kOutput, calls=%fused_computation.13 | convolution fusion | flops 14495514624 | bytes 41680896 | tf_op jit(solution)/shard_map/dot_general | solution.py:18
  155.3 35.0 %fusion.10 = f32[128,1536]{1,0:T(8,128)S(1)} fusion(f32[2,1536,6144]{2,1,0:T(8,128)} %param.6, f32[1,2,6144,128]{3,2,1,0:T(8,128)S(1)} %copy-done.2), kind=kOutput, calls=%fused_computation.15 | convolution fusion | flops 14495514624 | bytes 41680896 | tf_op jit(solution)/shard_map/dot_general | solution.py:18
  190.3 35.3 %fusion.73 = f32[1,1536,128]{1,2,0:T(8,128)S(1)} fusion(f32[128,1536]{1,0:T(8,128)S(1)} %fusion.8, f32[2,1536,6144]{2,1,0:T(8,128)} %param.6, f32[1,2,6144,128]{3,2,1,0:T(8,128)S(1)} %copy-done.2), kind=kOutput, calls=%fused_computation.79 | convolution fusion | flops 14495711232 | bytes 42467328 | tf_op jit(solution)/shard_map/dot_general | solution.py:18
  225.6 35.6 %fusion.67 = f32[1,1536,128]{1,2,0:T(8,128)S(1)} fusion(f32[128,1536]{1,0:T(8,128)S(1)} %fusion.10, f32[2,1536,6144]{2,1,0:T(8,128)} %param.6, f32[1,2,6144,128]{3,2,1,0:T(8,128)S(1)} %copy-done.2), kind=kOutput, calls=%fused_computation.77 | convolution fusion | flops 14495711232 | bytes 42467328 | tf_op jit(solution)/shard_map/dot_general | solution.py:18
  261.3 36.6 %fusion.4 = f32[128,1536]{1,0:T(8,128)S(1)} fusion(f32[2,1536,6144]{2,1,0:T(8,128)} %param.6, f32[1,2,6144,128]{3,2,1,0:T(8,128)} %all-gather.13.cloned.1.call-done), kind=kOutput, calls=%fused_computation.9 | convolution fusion | flops 14495514624 | bytes 41680896 | tf_op jit(solution)/shard_map/dot_general | solution.py:18
  297.9 35.2 %fusion.6 = f32[128,1536]{1,0:T(8,128)S(1)} fusion(f32[2,1536,6144]{2,1,0:T(8,128)} %param.6, f32[1,2,6144,128]{3,2,1,0:T(8,128)S(1)} %copy-done.3), kind=kOutput, calls=%fused_computation.11 | convolution fusion | flops 14495514624 | bytes 41680896 | tf_op jit(solution)/shard_map/dot_general | solution.py:18
  333.0 1.3 pad_maximum_fusion.3
  334.4 35.2 %fusion.85 = f32[1,1536,128]{1,2,0:T(8,128)S(1)} fusion(f32[128,1536]{1,0:T(8,128)S(1)} %fusion.4, f32[2,1536,6144]{2,1,0:T(8,128)} %param.6, f32[1,2,6144,128]{3,2,1,0:T(8,128)S(1)} %copy-done.3), kind=kOutput, calls=%fused_computation.83 | convolution fusion | flops 14495711232 | bytes 42467328 | tf_op jit(solution)/shard_map/dot_general | solution.py:18
  369.6 35.0 %fusion.79 = f32[1,1536,128]{1,2,0:T(8,128)S(1)} fusion(f32[128,1536]{1,0:T(8,128)S(1)} %fusion.6, f32[2,1536,6144]{2,1,0:T(8,128)} %param.6, f32[1,2,6144,128]{3,2,1,0:T(8,128)S(1)} %copy-done.3), kind=kOutput, calls=%fused_computation.81 | convolution fusion | flops 14495711232 | bytes 42467328 | tf_op jit(solution)/shard_map/dot_general | solution.py:18
  404.7 1.3 pad_maximum_fusion.4
  405.9 36.3 %fusion = f32[128,1536]{1,0:T(8,128)S(1)} fusion(f32[2,1536,6144]{2,1,0:T(8,128)} %param.6, f32[1,2,6144,128]{3,2,1,0:T(8,128)} %all-gather.15.cloned.1.call-done), kind=kOutput, calls=%fused_computation.5 | convolution fusion | flops 14495514624 | bytes 41680896 | tf_op jit(solution)/shard_map/dot_general | solution.py:18
  442.3 35.0 %fusion.2 = f32[128,1536]{1,0:T(8,128)S(1)} fusion(f32[2,1536,6144]{2,1,0:T(8,128)} %param.6, f32[1,2,6144,128]{3,2,1,0:T(8,128)S(1)} %copy-done.4), kind=kOutput, calls=%fused_computation.7 | convolution fusion | flops 14495514624 | bytes 41680896 | tf_op jit(solution)/shard_map/dot_general | solution.py:18
  477.3 35.5 %fusion.97 = f32[1,1536,128]{1,2,0:T(8,128)S(1)} fusion(f32[128,1536]{1,0:T(8,128)S(1)} %fusion, f32[2,1536,6144]{2,1,0:T(8,128)} %param.6, f32[1,2,6144,128]{3,2,1,0:T(8,128)S(1)} %copy-done.4), kind=kOutput, calls=%fused_computation.87 | convolution fusion | flops 14495711232 | bytes 42467328 | tf_op jit(solution)/shard_map/dot_general | solution.py:18
  512.8 35.0 %fusion.91 = f32[1,1536,128]{1,2,0:T(8,128)S(1)} fusion(f32[128,1536]{1,0:T(8,128)S(1)} %fusion.2, f32[2,1536,6144]{2,1,0:T(8,128)} %param.6, f32[1,2,6144,128]{3,2,1,0:T(8,128)S(1)} %copy-done.4), kind=kOutput, calls=%fused_computation.85 | convolution fusion | flops 14495711232 | bytes 42467328 | tf_op jit(solution)/shard_map/dot_general | solution.py:18
  547.9 1.2 pad_maximum_fusion.5
  549.1 36.3 %fusion.12 = f32[128,1536]{1,0:T(8,128)S(1)} fusion(f32[2,1536,6144]{2,1,0:T(8,128)} %param.6, f32[1,2,6144,128]{3,2,1,0:T(8,128)} %all-gather.9.cloned.1.call-done), kind=kOutput, calls=%fused_computation.17 | convolution fusion | flops 14495514624 | bytes 41680896 | tf_op jit(solution)/shard_map/dot_general | solution.py:18
  585.4 35.0 %fusion.14 = f32[128,1536]{1,0:T(8,128)S(1)} fusion(f32[2,1536,6144]{2,1,0:T(8,128)} %param.6, f32[1,2,6144,128]{3,2,1,0:T(8,128)S(1)} %copy-done.5), kind=kOutput, calls=%fused_computation.19 | convolution fusion | flops 14495514624 | bytes 41680896 | tf_op jit(solution)/shard_map/dot_general | solution.py:18
  620.5 35.5 %fusion.61 = f32[1,1536,128]{1,2,0:T(8,128)S(1)} fusion(f32[128,1536]{1,0:T(8,128)S(1)} %fusion.12, f32[2,1536,6144]{2,1,0:T(8,128)} %param.6, f32[1,2,6144,128]{3,2,1,0:T(8,128)S(1)} %copy-done.5), kind=kOutput, calls=%fused_computation.75 | convolution fusion | flops 14495711232 | bytes 42467328 | tf_op jit(solution)/shard_map/dot_general | solution.py:18
  655.9 35.0 %fusion.55 = f32[1,1536,128]{1,2,0:T(8,128)S(1)} fusion(f32[128,1536]{1,0:T(8,128)S(1)} %fusion.14, f32[2,1536,6144]{2,1,0:T(8,128)} %param.6, f32[1,2,6144,128]{3,2,1,0:T(8,128)S(1)} %copy-done.5), kind=kOutput, calls=%fused_computation.73 | convolution fusion | flops 14495711232 | bytes 42467328 | tf_op jit(solution)/shard_map/dot_general | solution.py:18
  691.0 1.3 pad_maximum_fusion.2
  692.4 1.6 dynamic-slice_multiply_fusion.2
  694.0 2.2 dynamic-slice_multiply_fusion.1
  696.2 2.3 dynamic-slice_multiply_fusion
  698.5 2.5 dynamic-slice_multiply_fusion.3
  701.1 2.9 pad_maximum_fusion.1
  704.5 1.7 gather_fusion.2
  708.2 1.5 broadcast_select_fusion
  709.7 13.4 %all-reduce.7.cloned.1.call-done = (f32[2,1536,128]{1,2,0:T(8,128)}, f32[2,1536,128]{1,2,0:T(8,128)}, f32[2,1536,128]{1,2,0:T(8,128)}, f32[2,1536,128]{1,2,0:T(8,128)}) async-done(((f32[2,1536,128]{1,2,0:T(8,128)}, f32[2,1536,128]{1,2,0:T(8,128)}, f32[2,1536,128]{1,2,0:T(8,128)}, f32[2,1536,128]{1,2,0:T(8,128)}), (f32[2,1536,128]{1,2,0:T(8,128)}, f32[2,1536,128]{1,2,0:T(8,128)}, f32[2,1536,128]{1,2,0:T(8,128)}, ...) | async-done | bytes 6291472 | tf_op jit(solution)/shard_map/psum | solution.py:66
  723.1 1.7 broadcast_multiply_fusion
  725.3 0.8 fusion.121
  726.2 0.8 fusion.122
  727.0 0.8 fusion.119
  727.9 0.8 fusion.120
  728.8 1.4 fusion.225
  730.2 1.4 fusion.224
  732.7 3.3 fusion.220
  737.4 0.8 fusion.127
  738.2 0.8 fusion.125
  740.9 0.9 fusion.51
  741.8 0.9 fusion.50
  742.7 0.9 fusion.49
  743.7 0.9 fusion.48
  746.2 0.8 fusion.135
  751.4 0.8 fusion.115
  753.0 0.8 fusion.117
  755.7 0.8 fusion.107
  757.3 0.8 fusion.109
  760.0 0.8 pad_maximum_fusion.6
  760.9 4.3 pad_maximum_fusion
  765.2 6.6 copy.33
  771.8 3.2 broadcast_in_dim.45
  775.0 13.3 %scatter_fusion = f32[4,2,1536,128]{3,2,1,0:T(8,128)} fusion(f32[4,2,1536,128]{3,2,1,0:T(8,128)} %broadcast_in_dim.45, s32[4]{0:T(128)S(1)} %copy-done.32, f32[4,2,1536,128]{3,2,1,0:T(8,128)} %copy.33), kind=kCustom, calls=%fused_computation.3 | custom fusion | bytes 18874384 | tf_op jit(solution)/shard_map/scatter | solution.py:118
  788.3 66.6 %all-reduce.5.cloned.1.call-done = (f32[4,2,128,128]{3,2,1,0:T(8,128)}, f32[2,2,128,128]{3,2,1,0:T(8,128)}) async-done(((f32[4,2,128,128]{3,2,1,0:T(8,128)}, f32[2,2,128,128]{3,2,1,0:T(8,128)}), (f32[4,2,128,128]{3,2,1,0:T(8,128)}, f32[2,2,128,128]{3,2,1,0:T(8,128)})) %all-reduce.5.cloned.1.call-update) | async-done | bytes 786448 | tf_op jit(solution)/shard_map/psum | solution.py:104
  854.9 1.1 slice_subtract_fusion.3
  857.7 1.0 fusion.140
  861.9 0.8 pad_maximum_fusion.7
  862.7 0.8 broadcast_in_dim.51
  863.6 2.7 scatter_fusion.1
  (151 shorter events, 27.0 us)
Async XLA Ops:
  7.2 3.5 copy-start
  7.2 112.0 %all-gather.11.cloned.1.call-start = ((), (), s32[]{:S(2)}) async-start(), calls=%async_computation.1 | async-start | bytes 7077888 | tf_op jit(solution)/shard_map/all_gather | solution.py:64
  8.0 5.4 copy-start.33
  8.8 0.5 copy-start.31
  9.3 3.8 copy-start.30
  10.6 2.4 copy-start.34
  10.6 2.4 copy-start.36
  17.6 243.7 %all-gather.13.cloned.1.call-start = ((), (), s32[]{:S(2)}) async-start(), calls=%async_computation.2 | async-start | bytes 7077888 | tf_op jit(solution)/shard_map/all_gather | solution.py:64
  18.3 387.6 %all-gather.15.cloned.1.call-start = ((), (), s32[]{:S(2)}) async-start(), calls=%async_computation.3 | async-start | bytes 7077888 | tf_op jit(solution)/shard_map/all_gather | solution.py:64
  19.1 530.0 %all-gather.9.cloned.1.call-start = ((), (), s32[]{:S(2)}) async-start(), calls=%async_computation | async-start | bytes 7077888 | tf_op jit(solution)/shard_map/all_gather | solution.py:64
  19.7 703.5 %all-reduce.7.cloned.1.call-start = ((), (), s32[]{:S(2)}) async-start(), calls=%async_computation.5 | async-start | bytes 12582912 | tf_op jit(solution)/shard_map/psum | solution.py:66
  119.2 36.1 %copy-start.2 = (f32[1,2,6144,128]{3,2,1,0:T(8,128)S(1)}, f32[1,2,6144,128]{3,2,1,0:T(8,128)}, u32[]{:S(2)}) copy-start(f32[1,2,6144,128]{3,2,1,0:T(8,128)} %all-gather.11.cloned.1.call-done) | copy-start | bytes 18874372
  261.3 36.6 %copy-start.3 = (f32[1,2,6144,128]{3,2,1,0:T(8,128)S(1)}, f32[1,2,6144,128]{3,2,1,0:T(8,128)}, u32[]{:S(2)}) copy-start(f32[1,2,6144,128]{3,2,1,0:T(8,128)} %all-gather.13.cloned.1.call-done) | copy-start | bytes 18874372
  405.9 36.3 %copy-start.4 = (f32[1,2,6144,128]{3,2,1,0:T(8,128)S(1)}, f32[1,2,6144,128]{3,2,1,0:T(8,128)}, u32[]{:S(2)}) copy-start(f32[1,2,6144,128]{3,2,1,0:T(8,128)} %all-gather.15.cloned.1.call-done) | copy-start | bytes 18874372
  549.1 36.3 %copy-start.5 = (f32[1,2,6144,128]{3,2,1,0:T(8,128)S(1)}, f32[1,2,6144,128]{3,2,1,0:T(8,128)}, u32[]{:S(2)}) copy-start(f32[1,2,6144,128]{3,2,1,0:T(8,128)} %all-gather.9.cloned.1.call-done) | copy-start | bytes 18874372
  692.3 162.6 %all-reduce.5.cloned.1.call-start = ((), (), s32[]{:S(2)}) async-start(), calls=%async_computation.4 | async-start | bytes 1572864 | tf_op jit(solution)/shard_map/psum | solution.py:104
  694.0 7.1 copy-start.10
  696.2 4.9 copy-start.12
  698.5 5.5 copy-start.14
  701.1 3.4 copy-start.16
  701.1 5.2 copy-start.35
  701.1 5.2 copy-start.37
  701.1 6.4 copy-start.18
  704.5 27.2 %collective-permute-start = (f32[4,2,1536,128]{3,2,1,0:T(8,128)}, f32[4,2,1536,128]{3,2,1,0:T(8,128)}, u32[]{:S(2)}, u32[]{:S(2)}) collective-permute-start(f32[4,2,1536,128]{3,2,1,0:T(8,128)} %pad_maximum_fusion.1), channel_id=1, source_target_pairs={{0,1},{1,0},{2,3},{3,2},{4,5},{5,4},{6,7},{7,6},{8,9},{9,8},{10,11... | collective-permute-start | bytes 18874376 | tf_op jit(solution)/shard_map/ppermute | solution.py:14
  723.1 1.9 copy-start.19
  725.3 3.4 copy-start.20
  728.8 2.9 copy-start.11
  728.8 2.9 copy-start.13
  728.8 3.5 copy-start.15
  728.8 3.9 copy-start.17
  743.6 1.4 copy-start.23
  743.6 1.9 copy-start.24
  743.6 1.9 copy-start.28
  743.7 1.9 copy-start.29
  746.2 9.5 %copy-start.8 = (f32[2,1536,128]{1,2,0:T(8,128)}, f32[2,1536,128]{1,2,0:T(8,128)S(1)}, u32[]{:S(2)}) copy-start(f32[2,1536,128]{1,2,0:T(8,128)S(1)} %get-tuple-element.36) | copy-start | bytes 4718596
  746.2 11.1 %copy-start.6 = (f32[2,1536,128]{1,2,0:T(8,128)}, f32[2,1536,128]{1,2,0:T(8,128)S(1)}, u32[]{:S(2)}) copy-start(f32[2,1536,128]{1,2,0:T(8,128)S(1)} %get-tuple-element.35) | copy-start | bytes 4718596
  757.3 3.5 copy-start.9
  758.1 2.7 copy-start.7
  771.8 3.2 copy-start.32
  775.0 79.9 %copy-start.21 = (f32[4,2,128,128]{3,2,1,0:T(8,128)S(1)}, f32[4,2,128,128]{3,2,1,0:T(8,128)}, u32[]{:S(2)}) copy-start(f32[4,2,128,128]{3,2,1,0:T(8,128)} %broadcast_select_fusion) | copy-start | bytes 1572868
  788.3 70.4 %copy-start.26 = (f32[2,128,128]{1,2,0:T(8,128)S(1)}, f32[2,128,128]{1,2,0:T(8,128)}, u32[]{:S(2)}) copy-start(f32[2,128,128]{1,2,0:T(8,128)} %get-tuple-element.31) | copy-start | bytes 393220
  854.9 5.0 copy-start.27
  854.9 6.2 copy-start.22
  854.9 6.2 copy-start.25
  859.9 6.4 copy-start.1
Sparse Core Ops, SparseCore 0:
  17.7 101.4 all-gather.10
  121.4 96.8 all-gather.12
  220.5 96.9 all-gather.14
  320.1 96.8 all-gather.8
  692.4 30.6 all-reduce.6
  761.0 93.8 all-reduce.4
where the time goes:
time: 883 us; the launch traced here: 874 us
  matrix products  597 us (68%)
  waiting for transfers between devices  181 us (20%)
  other arithmetic  41.3 us (5%)
  local copies, waits for them, and re-layouts  38.3 us (4%)
  between operations  15.6 us (2%)
    dot_general x66, matrix products, matmul(): jnp.dot(left_side, right_side, preferred_element_type=jnp.float32, precis...  597 us
    all_gather x4, waiting for transfers between devices, per_device(): gathered = lax.all_gather(panels[tree_slot], 'row', axis=1, tiled=True)  99.5 us
    psum x1, waiting for transfers between devices, per_device(): lax.psum(jnp.stack(cross_local + child_local), ('row', 'col'))  66.6 us
  transfers between devices with their start and end apart: 7, of which 3 were waited for; matrix products, arithmetic and copies ran while one was open for 55% of the time, Pallas kernels for 0%

commit v1 on v0

--- a/solution.py
+++ b/solution.py
@@ -101,7 +101,7 @@
     ]
     parent_sums = lax.psum(jnp.stack(parent_local), ("row", "col"))
     parent_diag = [diag_blocks[tree_slot] - parent_sums[tree_slot] for tree_slot in range(2)]
-    child_totals = lax.psum(jnp.stack(cross_local + child_local), ("row", "col"))
+    child_totals = lax.psum(lax.psum(jnp.stack(cross_local + child_local), "col"), "row")
     crosses = [
         -(child_totals[tree_slot] + multiply(parent_diag[tree_slot], coupling[tree_slot]))
         for tree_slot in range(2)

time: 883 us -> 978 us (1.11)
  waiting for transfers between devices: 181 us -> 264 us
  matrix products: 597 us -> 610 us
    psum x1 -> x3, waiting for transfers between devices: 66.6 us -> 148 us  [the longest x1 76.6 us: per_device(): lax.psum(lax.psum(jnp.stack(cross_local + child_local), 'col'), 'row')]
    dot_general x66, matrix products: 597 us -> 610 us  [matmul(): jnp.dot(left_side, right_side, preferred_element_type=jnp.float32, precis...]
  transfers between devices with their start and end apart: 7 -> 9, of which waited for: 3 -> 5; matrix products, arithmetic and copies ran while one was open for 55% -> 51% of each run, Pallas kernels for 0% -> 0%
where the time goes in v1:
time: 978 us; the launch traced here: 969 us
  matrix products  610 us (62%)
  waiting for transfers between devices  264 us (27%)
  other arithmetic  41 us (4%)
  local copies, waits for them, and re-layouts  38.2 us (4%)
  between operations  15.8 us (2%)
    dot_general x66, matrix products, matmul(): jnp.dot(left_side, right_side, preferred_element_type=jnp.float32, precis...  610 us
    all_gather x4, waiting for transfers between devices, per_device(): gathered = lax.all_gather(panels[tree_slot], 'row', axis=1, tiled=True)  99.5 us
    psum x1, waiting for transfers between devices, per_device(): lax.psum(lax.psum(jnp.stack(cross_local + child_local), 'col'), 'row')  76.6 us
    psum x1, waiting for transfers between devices, per_device(): parent_sums = lax.psum(jnp.stack(parent_local), ('row', 'col'))  51.7 us
  transfers between devices with their start and end apart: 9, of which 5 were waited for; matrix products, arithmetic and copies ran while one was open for 51% of the time, Pallas kernels for 0%

profile of v1, /device:TPU:0, one launch (start us, length us, event | category | flops | bytes accessed | tf_op | source)
XLA Modules:
  0.0 969.0 jit_solution(15299070539994922334)
XLA Ops:
  9.4 1.2 gather_fusion
  10.7 2.4 gather_fusion.1
  13.5 2.4 select_multiply_fusion
  15.9 1.7 fusion.222
  19.8 99.5 %all-gather.11.cloned.1.call-done = f32[1,2,6144,128]{3,2,1,0:T(8,128)} async-done(((f32[1,2,768,128]{3,2,1,0:T(8,128)}), f32[1,2,6144,128]{3,2,1,0:T(8,128)}) %all-gather.11.cloned.1.call-update) | async-done | bytes 6291472 | tf_op jit(solution)/shard_map/all_gather | solution.py:64
  119.2 36.1 %fusion.8 = f32[128,1536]{1,0:T(8,128)S(1)} fusion(f32[2,1536,6144]{2,1,0:T(8,128)} %param.6, f32[1,2,6144,128]{3,2,1,0:T(8,128)} %all-gather.11.cloned.1.call-done), kind=kOutput, calls=%fused_computation.13 | convolution fusion | flops 14495514624 | bytes 41680896 | tf_op jit(solution)/shard_map/dot_general | solution.py:18
  155.3 35.0 %fusion.10 = f32[128,1536]{1,0:T(8,128)S(1)} fusion(f32[2,1536,6144]{2,1,0:T(8,128)} %param.6, f32[1,2,6144,128]{3,2,1,0:T(8,128)S(1)} %copy-done.2), kind=kOutput, calls=%fused_computation.15 | convolution fusion | flops 14495514624 | bytes 41680896 | tf_op jit(solution)/shard_map/dot_general | solution.py:18
  190.4 35.3 %fusion.73 = f32[1,1536,128]{1,2,0:T(8,128)S(1)} fusion(f32[128,1536]{1,0:T(8,128)S(1)} %fusion.8, f32[2,1536,6144]{2,1,0:T(8,128)} %param.6, f32[1,2,6144,128]{3,2,1,0:T(8,128)S(1)} %copy-done.2), kind=kOutput, calls=%fused_computation.79 | convolution fusion | flops 14495711232 | bytes 42467328 | tf_op jit(solution)/shard_map/dot_general | solution.py:18
  225.7 35.6 %fusion.67 = f32[1,1536,128]{1,2,0:T(8,128)S(1)} fusion(f32[128,1536]{1,0:T(8,128)S(1)} %fusion.10, f32[2,1536,6144]{2,1,0:T(8,128)} %param.6, f32[1,2,6144,128]{3,2,1,0:T(8,128)S(1)} %copy-done.2), kind=kOutput, calls=%fused_computation.77 | convolution fusion | flops 14495711232 | bytes 42467328 | tf_op jit(solution)/shard_map/dot_general | solution.py:18
  261.3 36.5 %fusion.4 = f32[128,1536]{1,0:T(8,128)S(1)} fusion(f32[2,1536,6144]{2,1,0:T(8,128)} %param.6, f32[1,2,6144,128]{3,2,1,0:T(8,128)} %all-gather.13.cloned.1.call-done), kind=kOutput, calls=%fused_computation.9 | convolution fusion | flops 14495514624 | bytes 41680896 | tf_op jit(solution)/shard_map/dot_general | solution.py:18
  297.9 35.2 %fusion.6 = f32[128,1536]{1,0:T(8,128)S(1)} fusion(f32[2,1536,6144]{2,1,0:T(8,128)} %param.6, f32[1,2,6144,128]{3,2,1,0:T(8,128)S(1)} %copy-done.3), kind=kOutput, calls=%fused_computation.11 | convolution fusion | flops 14495514624 | bytes 41680896 | tf_op jit(solution)/shard_map/dot_general | solution.py:18
  333.1 1.3 pad_maximum_fusion.3
  334.4 35.2 %fusion.85 = f32[1,1536,128]{1,2,0:T(8,128)S(1)} fusion(f32[128,1536]{1,0:T(8,128)S(1)} %fusion.4, f32[2,1536,6144]{2,1,0:T(8,128)} %param.6, f32[1,2,6144,128]{3,2,1,0:T(8,128)S(1)} %copy-done.3), kind=kOutput, calls=%fused_computation.83 | convolution fusion | flops 14495711232 | bytes 42467328 | tf_op jit(solution)/shard_map/dot_general | solution.py:18
  369.6 35.1 %fusion.79 = f32[1,1536,128]{1,2,0:T(8,128)S(1)} fusion(f32[128,1536]{1,0:T(8,128)S(1)} %fusion.6, f32[2,1536,6144]{2,1,0:T(8,128)} %param.6, f32[1,2,6144,128]{3,2,1,0:T(8,128)S(1)} %copy-done.3), kind=kOutput, calls=%fused_computation.81 | convolution fusion | flops 14495711232 | bytes 42467328 | tf_op jit(solution)/shard_map/dot_general | solution.py:18
  404.6 1.3 pad_maximum_fusion.4
  405.9 36.3 %fusion = f32[128,1536]{1,0:T(8,128)S(1)} fusion(f32[2,1536,6144]{2,1,0:T(8,128)} %param.6, f32[1,2,6144,128]{3,2,1,0:T(8,128)} %all-gather.15.cloned.1.call-done), kind=kOutput, calls=%fused_computation.5 | convolution fusion | flops 14495514624 | bytes 41680896 | tf_op jit(solution)/shard_map/dot_general | solution.py:18
  442.2 35.0 %fusion.2 = f32[128,1536]{1,0:T(8,128)S(1)} fusion(f32[2,1536,6144]{2,1,0:T(8,128)} %param.6, f32[1,2,6144,128]{3,2,1,0:T(8,128)S(1)} %copy-done.4), kind=kOutput, calls=%fused_computation.7 | convolution fusion | flops 14495514624 | bytes 41680896 | tf_op jit(solution)/shard_map/dot_general | solution.py:18
  477.3 35.5 %fusion.97 = f32[1,1536,128]{1,2,0:T(8,128)S(1)} fusion(f32[128,1536]{1,0:T(8,128)S(1)} %fusion, f32[2,1536,6144]{2,1,0:T(8,128)} %param.6, f32[1,2,6144,128]{3,2,1,0:T(8,128)S(1)} %copy-done.4), kind=kOutput, calls=%fused_computation.87 | convolution fusion | flops 14495711232 | bytes 42467328 | tf_op jit(solution)/shard_map/dot_general | solution.py:18
  512.7 35.0 %fusion.91 = f32[1,1536,128]{1,2,0:T(8,128)S(1)} fusion(f32[128,1536]{1,0:T(8,128)S(1)} %fusion.2, f32[2,1536,6144]{2,1,0:T(8,128)} %param.6, f32[1,2,6144,128]{3,2,1,0:T(8,128)S(1)} %copy-done.4), kind=kOutput, calls=%fused_computation.85 | convolution fusion | flops 14495711232 | bytes 42467328 | tf_op jit(solution)/shard_map/dot_general | solution.py:18
  547.8 1.3 pad_maximum_fusion.5
  549.0 36.3 %fusion.12 = f32[128,1536]{1,0:T(8,128)S(1)} fusion(f32[2,1536,6144]{2,1,0:T(8,128)} %param.6, f32[1,2,6144,128]{3,2,1,0:T(8,128)} %all-gather.9.cloned.1.call-done), kind=kOutput, calls=%fused_computation.17 | convolution fusion | flops 14495514624 | bytes 41680896 | tf_op jit(solution)/shard_map/dot_general | solution.py:18
  585.3 35.0 %fusion.14 = f32[128,1536]{1,0:T(8,128)S(1)} fusion(f32[2,1536,6144]{2,1,0:T(8,128)} %param.6, f32[1,2,6144,128]{3,2,1,0:T(8,128)S(1)} %copy-done.5), kind=kOutput, calls=%fused_computation.19 | convolution fusion | flops 14495514624 | bytes 41680896 | tf_op jit(solution)/shard_map/dot_general | solution.py:18
  620.4 35.5 %fusion.61 = f32[1,1536,128]{1,2,0:T(8,128)S(1)} fusion(f32[128,1536]{1,0:T(8,128)S(1)} %fusion.12, f32[2,1536,6144]{2,1,0:T(8,128)} %param.6, f32[1,2,6144,128]{3,2,1,0:T(8,128)S(1)} %copy-done.5), kind=kOutput, calls=%fused_computation.75 | convolution fusion | flops 14495711232 | bytes 42467328 | tf_op jit(solution)/shard_map/dot_general | solution.py:18
  655.9 35.0 %fusion.55 = f32[1,1536,128]{1,2,0:T(8,128)S(1)} fusion(f32[128,1536]{1,0:T(8,128)S(1)} %fusion.14, f32[2,1536,6144]{2,1,0:T(8,128)} %param.6, f32[1,2,6144,128]{3,2,1,0:T(8,128)S(1)} %copy-done.5), kind=kOutput, calls=%fused_computation.73 | convolution fusion | flops 14495711232 | bytes 42467328 | tf_op jit(solution)/shard_map/dot_general | solution.py:18
  690.9 1.3 pad_maximum_fusion.2
  692.3 1.6 dynamic-slice_multiply_fusion.2
  693.9 2.2 dynamic-slice_multiply_fusion.1
  696.1 2.3 dynamic-slice_multiply_fusion
  698.4 2.5 dynamic-slice_multiply_fusion.3
  701.0 2.9 pad_maximum_fusion.1
  704.3 1.7 gather_fusion.2
  708.4 14.6 %all-reduce.12.cloned.1.call-done = (f32[2,1536,128]{1,2,0:T(8,128)}, f32[2,1536,128]{1,2,0:T(8,128)}, f32[2,1536,128]{1,2,0:T(8,128)}, f32[2,1536,128]{1,2,0:T(8,128)}) async-done(((f32[2,1536,128]{1,2,0:T(8,128)}, f32[2,1536,128]{1,2,0:T(8,128)}, f32[2,1536,128]{1,2,0:T(8,128)}, f32[2,1536,128]{1,2,0:T(8,128)}), (f32[2,1536,128]{1,2,0:T(8,128)}, f32[2,1536,128]{1,2,0:T(8,128)}, f32[2,1536,128]{1,2,0:T(8,128)}, ...) | async-done | bytes 6291472 | tf_op jit(solution)/shard_map/psum | solution.py:66
  723.0 1.7 broadcast_multiply_fusion
  728.7 1.4 fusion.225
  730.1 1.4 fusion.224
  732.7 3.3 fusion.220
  740.3 1.1 fusion.132
  743.3 0.9 fusion.49
  744.2 0.9 fusion.48
  746.8 1.6 fusion.135
  748.4 1.4 fusion.136
  749.8 1.4 fusion.133
  751.2 1.6 fusion.134
  753.4 1.1 fusion.130
  758.6 1.8 fusion.110
  760.4 1.6 fusion.111
  762.1 1.9 fusion.106
  764.0 1.8 fusion.107
  765.8 1.8 fusion.108
  770.9 2.9 pad_maximum_fusion
  773.8 6.6 copy.33
  780.4 3.2 broadcast_in_dim.45
  783.6 13.1 %scatter_fusion = f32[4,2,1536,128]{3,2,1,0:T(8,128)} fusion(f32[4,2,1536,128]{3,2,1,0:T(8,128)} %broadcast_in_dim.45, s32[4]{0:T(128)S(1)} %copy-done.49, f32[4,2,1536,128]{3,2,1,0:T(8,128)} %copy.33), kind=kCustom, calls=%fused_computation.3 | custom fusion | bytes 18874384 | tf_op jit(solution)/shard_map/scatter | solution.py:118
  797.9 51.7 %all-reduce.6.cloned.1.call-done = f32[2,2,128,128]{3,2,1,0:T(8,128)} async-done(((f32[2,2,128,128]{3,2,1,0:T(8,128)}), f32[2,2,128,128]{3,2,1,0:T(8,128)}) %all-reduce.6.cloned.1.call-update) | async-done | bytes 262160 | tf_op jit(solution)/shard_map/psum | solution.py:102
  849.6 1.0 slice_subtract_fusion.3
  851.6 19.4 %all-reduce.8.cloned.1.call-done = f32[4,2,128,128]{3,2,1,0:T(8,128)} async-done(((f32[4,2,128,128]{3,2,1,0:T(8,128)}), f32[4,2,128,128]{3,2,1,0:T(8,128)}) %all-reduce.8.cloned.1.call-update) | async-done | bytes 524304 | tf_op jit(solution)/shard_map/psum | solution.py:104
  871.7 76.6 %all-reduce.10.cloned.1.call-done = f32[4,2,128,128]{3,2,1,0:T(8,128)} async-done(((f32[4,2,128,128]{3,2,1,0:T(8,128)}), f32[4,2,128,128]{3,2,1,0:T(8,128)}) %all-reduce.10.cloned.1.call-update) | async-done | bytes 524304 | tf_op jit(solution)/shard_map/psum | solution.py:104
  948.3 1.0 fusion.140
  950.6 1.3 fusion.104
  951.9 1.1 fusion.105
  953.0 1.1 fusion.102
  954.2 1.1 fusion.103
  955.3 1.4 fusion.142
  959.1 2.7 scatter_fusion.1
  (193 shorter events, 34.3 us)
Async XLA Ops:
  7.2 3.6 copy-start
  7.2 112.1 %all-gather.11.cloned.1.call-start = ((), (), s32[]{:S(2)}) async-start(), calls=%async_computation.4 | async-start | bytes 7077888 | tf_op jit(solution)/shard_map/all_gather | solution.py:64
  8.0 5.5 copy-start.50
  9.4 3.8 copy-start.47
  10.7 2.4 copy-start.52
  10.7 2.4 copy-start.54
  17.7 243.7 %all-gather.13.cloned.1.call-start = ((), (), s32[]{:S(2)}) async-start(), calls=%async_computation.5 | async-start | bytes 7077888 | tf_op jit(solution)/shard_map/all_gather | solution.py:64
  18.4 387.5 %all-gather.15.cloned.1.call-start = ((), (), s32[]{:S(2)}) async-start(), calls=%async_computation.6 | async-start | bytes 7077888 | tf_op jit(solution)/shard_map/all_gather | solution.py:64
  19.1 529.9 %all-gather.9.cloned.1.call-start = ((), (), s32[]{:S(2)}) async-start(), calls=%async_computation.3 | async-start | bytes 7077888 | tf_op jit(solution)/shard_map/all_gather | solution.py:64
  19.7 703.3 %all-reduce.12.cloned.1.call-start = ((), (), s32[]{:S(2)}) async-start(), calls=%async_computation.7 | async-start | bytes 12582912 | tf_op jit(solution)/shard_map/psum | solution.py:66
  119.2 36.1 %copy-start.2 = (f32[1,2,6144,128]{3,2,1,0:T(8,128)S(1)}, f32[1,2,6144,128]{3,2,1,0:T(8,128)}, u32[]{:S(2)}) copy-start(f32[1,2,6144,128]{3,2,1,0:T(8,128)} %all-gather.11.cloned.1.call-done) | copy-start | bytes 18874372
  261.3 36.6 %copy-start.3 = (f32[1,2,6144,128]{3,2,1,0:T(8,128)S(1)}, f32[1,2,6144,128]{3,2,1,0:T(8,128)}, u32[]{:S(2)}) copy-start(f32[1,2,6144,128]{3,2,1,0:T(8,128)} %all-gather.13.cloned.1.call-done) | copy-start | bytes 18874372
  405.9 36.3 %copy-start.4 = (f32[1,2,6144,128]{3,2,1,0:T(8,128)S(1)}, f32[1,2,6144,128]{3,2,1,0:T(8,128)}, u32[]{:S(2)}) copy-start(f32[1,2,6144,128]{3,2,1,0:T(8,128)} %all-gather.15.cloned.1.call-done) | copy-start | bytes 18874372
  549.0 36.3 %copy-start.5 = (f32[1,2,6144,128]{3,2,1,0:T(8,128)S(1)}, f32[1,2,6144,128]{3,2,1,0:T(8,128)}, u32[]{:S(2)}) copy-start(f32[1,2,6144,128]{3,2,1,0:T(8,128)} %all-gather.9.cloned.1.call-done) | copy-start | bytes 18874372
  692.2 157.4 %all-reduce.6.cloned.1.call-start = ((), (), s32[]{:S(2)}) async-start(), calls=%async_computation | async-start | bytes 524288 | tf_op jit(solution)/shard_map/psum | solution.py:102
  693.9 7.1 copy-start.10
  696.0 4.9 copy-start.12
  698.4 5.5 copy-start.14
  700.9 3.4 copy-start.16
  701.0 5.2 copy-start.53
  701.0 5.2 copy-start.55
  701.0 5.8 copy-start.27
  701.0 6.5 copy-start.51
  704.3 27.2 %collective-permute-start = (f32[4,2,1536,128]{3,2,1,0:T(8,128)}, f32[4,2,1536,128]{3,2,1,0:T(8,128)}, u32[]{:S(2)}, u32[]{:S(2)}) collective-permute-start(f32[4,2,1536,128]{3,2,1,0:T(8,128)} %pad_maximum_fusion.1), channel_id=1, source_target_pairs={{0,1},{1,0},{2,3},{3,2},{4,5},{5,4},{6,7},{7,6},{8,9},{9,8},{10,11... | collective-permute-start | bytes 18874376 | tf_op jit(solution)/shard_map/ppermute | solution.py:14
  723.0 1.9 copy-start.30
  725.2 15.1 %copy-start.23 = (f32[2,128,768]{2,1,0:T(8,128)}, f32[2,128,768]{2,1,0:T(8,128)S(1)}, u32[]{:S(2)}) copy-start(f32[2,128,768]{2,1,0:T(8,128)S(1)} %get-tuple-element.39) | copy-start | bytes 2359300
  725.2 28.1 %copy-start.21 = (f32[2,128,768]{2,1,0:T(8,128)}, f32[2,128,768]{2,1,0:T(8,128)S(1)}, u32[]{:S(2)}) copy-start(f32[2,128,768]{2,1,0:T(8,128)S(1)} %get-tuple-element.40) | copy-start | bytes 2359300
  725.2 3.4 copy-start.31
  728.7 2.8 copy-start.11
  728.7 2.8 copy-start.13
  728.7 3.5 copy-start.15
  728.7 3.9 copy-start.17
  736.4 8.7 copy-start.20
  736.4 16.9 %copy-start.18 = (f32[1,2,1536,128]{3,2,1,0:T(8,128)}, f32[1,2,1536,128]{3,2,1,0:T(8,128)S(1)}, u32[]{:S(2)}) copy-start(f32[1,2,1536,128]{3,2,1,0:T(8,128)S(1)} %get-tuple-element.13) | copy-start | bytes 4718596
  744.2 1.4 copy-start.35
  744.2 1.9 copy-start.36
  745.3 3.1 copy-start.26
  745.3 6.0 copy-start.24
  746.7 9.4 copy-start.6
  746.8 9.4 copy-start.8
  756.9 8.9 copy-start.7
  757.7 4.3 copy-start.9
  758.5 112.5 %all-reduce.8.cloned.1.call-start = ((), (), s32[]{:S(2)}) async-start(), calls=%async_computation.1 | async-start | bytes 1048576 | tf_op jit(solution)/shard_map/psum | solution.py:104
  758.6 9.1 copy-start.25
  758.6 9.1 copy-start.45
  758.6 9.9 %copy-start.19 = (f32[1,2,1536,128]{3,2,1,0:T(8,128)S(1)}, f32[1,2,1536,128]{3,2,1,0:T(8,128)}, u32[]{:S(2)}) copy-start(f32[1,2,1536,128]{3,2,1,0:T(8,128)} %copy-done.18) | copy-start | bytes 4718596
  758.6 9.9 %copy-start.22 = (f32[2,128,768]{2,1,0:T(8,128)S(1)}, f32[2,128,768]{2,1,0:T(8,128)}, u32[]{:S(2)}) copy-start(f32[2,128,768]{2,1,0:T(8,128)} %copy-done.21) | copy-start | bytes 2359300
  758.6 10.4 %copy-start.46 = (f32[128,128]{1,0:T(8,128)S(1)}, f32[128,128]{1,0:T(8,128)}, u32[]{:S(2)}) copy-start(f32[128,128]{1,0:T(8,128)} %fusion.130) | copy-start | bytes 196612
  762.1 8.8 copy-start.28
  762.1 8.8 copy-start.29
  780.4 3.2 copy-start.49
  783.6 13.1 %copy-start.43 = (f32[1,2,128,128]{3,2,1,0:T(8,128)S(1)}, f32[1,2,128,128]{3,2,1,0:T(8,128)}, u32[]{:S(2)}) copy-start(f32[1,2,128,128]{3,2,1,0:T(8,128)} %maximum_bitcast_fusion.5) | copy-start | bytes 393220
  783.6 13.1 %copy-start.44 = (f32[1,2,128,128]{3,2,1,0:T(8,128)S(1)}, f32[1,2,128,128]{3,2,1,0:T(8,128)}, u32[]{:S(2)}) copy-start(f32[1,2,128,128]{3,2,1,0:T(8,128)} %maximum_bitcast_fusion.4) | copy-start | bytes 393220
  783.6 65.9 %copy-start.32 = (f32[4,2,128,128]{3,2,1,0:T(8,128)S(1)}, f32[4,2,128,128]{3,2,1,0:T(8,128)}, u32[]{:S(2)}) copy-start(f32[4,2,128,128]{3,2,1,0:T(8,128)} %broadcast_select_fusion) | copy-start | bytes 1572868
  796.7 152.7 %copy-start.38 = (f32[2,128,128]{1,2,0:T(8,128)S(1)}, f32[2,128,128]{1,2,0:T(8,128)}, u32[]{:S(2)}) copy-start(f32[2,128,128]{1,2,0:T(8,128)} %get-tuple-element.29) | copy-start | bytes 393220
  796.7 153.3 %copy-start.37 = (f32[2,128,128]{1,2,0:T(8,128)S(1)}, f32[2,128,128]{1,2,0:T(8,128)}, u32[]{:S(2)}) copy-start(f32[2,128,128]{1,2,0:T(8,128)} %get-tuple-element.30) | copy-start | bytes 393220
  797.6 150.8 %all-reduce.10.cloned.1.call-start = ((), (), s32[]{:S(2)}) async-start(), calls=%async_computation.2 | async-start | bytes 1048576 | tf_op jit(solution)/shard_map/psum | solution.py:104
  850.6 21.1 %copy-start.33 = (f32[1,2,128,128]{3,2,1,0:T(8,128)}, f32[1,2,128,128]{3,2,1,0:T(8,128)S(1)}, u32[]{:S(2)}) copy-start(f32[1,2,128,128]{3,2,1,0:T(8,128)S(1)} %get-tuple-element.22) | copy-start | bytes 393220
  851.4 98.6 %copy-start.39 = (f32[128,128]{1,0:T(8,128)}, f32[128,128]{1,0:T(8,128)S(1)}, u32[]{:S(2)}) copy-start(f32[128,128]{1,0:T(8,128)S(1)} %convolution_add_fusion.5) | copy-start | bytes 196612
  851.6 98.3 %copy-start.40 = (f32[128,128]{1,0:T(8,128)}, f32[128,128]{1,0:T(8,128)S(1)}, u32[]{:S(2)}) copy-start(f32[128,128]{1,0:T(8,128)S(1)} %convolution_subtract_fusion.5) | copy-start | bytes 196612
  871.5 78.5 %copy-start.41 = (f32[128,128]{1,0:T(8,128)}, f32[128,128]{1,0:T(8,128)S(1)}, u32[]{:S(2)}) copy-start(f32[128,128]{1,0:T(8,128)S(1)} %convolution_add_fusion.3) | copy-start | bytes 196612
  871.7 78.6 %copy-start.42 = (f32[128,128]{1,0:T(8,128)}, f32[128,128]{1,0:T(8,128)S(1)}, u32[]{:S(2)}) copy-start(f32[128,128]{1,0:T(8,128)S(1)} %convolution_subtract_fusion.3) | copy-start | bytes 196612
  948.3 9.1 copy-start.34
  950.6 11.2 %copy-start.1 = (f32[4,2,768,128]{3,2,1,0:T(8,128)S(1)}, f32[4,2,768,128]{3,2,1,0:T(8,128)}, u32[]{:S(2)}) copy-start(f32[4,2,768,128]{3,2,1,0:T(8,128)} %param.7) | copy-start | bytes 9437188
  (1 other events, 0.6 us)
Sparse Core Ops, SparseCore 0:
  17.8 101.4 all-gather.10
  121.4 96.8 all-gather.12
  220.5 96.9 all-gather.14
  320.1 96.8 all-gather.8
  692.3 30.6 all-reduce.11
  758.7 90.8 all-reduce.5
  851.9 19.0 all-reduce.7
  874.4 73.8 all-reduce.9
